TPU v7x, 32 devices: a whole 2x2x4 slice. The times are simulated.
32 devices in a mesh: vec: 8 (over z, core), rep: 4 (over y, x).
Axes of the slice: x: 2, y: 2, z: 4, core: 2. Of those that a mesh axis runs over, the one named last changes fastest.
Arguments:
- vectors: bfloat16 [1024, 1024], P('vec'), may hold values from 0 to 2
- pivot_index: int32 [4, 8], P('rep'), may hold values from 0 to 1023
Outputs:
- similarity: bfloat16 [7, 32, 1024, 128], P(None, 'rep', 'vec')
All inputs are finite; a program needn't handle non-finite values.
Results may differ from a plain program's by a relative error of at most 0.011.
Values may be sent and summed in bfloat16 or wider, within the bound.
A program may use at most 64 MiB of HBM per device.

v0:
```python
import math
import jax
import jax.numpy as jnp
from jax import lax
from jax.sharding import PartitionSpec as P

HALF = 3


def from_behind(block, axis, distance):
    devices = range(lax.axis_size(axis))
    route = [((i - distance) % len(devices), i) for i in devices]
    return lax.ppermute(block, axis, route)


def contract(left, right):
    return lax.dot_general(
        left, right, (((1,), (1,)), ((), ())), preferred_element_type=jnp.float32
    )


def on_device(vectors, pivot_index):
    block_rows, fields = vectors.shape
    position = lax.axis_index("vec")
    wanted = pivot_index.reshape(-1) - position * block_rows
    columns = jnp.arange(block_rows, dtype=jnp.int32)
    onehot = (wanted[:, None] == columns[None, :]).astype(jnp.bfloat16)
    local_rows = jnp.dot(onehot, vectors, preferred_element_type=jnp.float32)
    pivots = lax.psum(local_rows, "vec")
    count = pivots.shape[0]
    centre = jnp.sum(pivots, axis=1) / fields
    scaled = (vectors.astype(jnp.float32)[None, :, :] * pivots[:, None, :]).astype(jnp.bfloat16)
    scaled = scaled.reshape(count * block_rows, fields)
    replicas = lax.axis_size("rep")
    share = block_rows // replicas
    own_rows = lax.dynamic_slice_in_dim(vectors, lax.axis_index("rep") * share, share, 0)
    window = 2 * HALF + 1
    triples = [None] * window
    grams = [None] * window
    triples[HALF] = contract(scaled, vectors)
    grams[HALF] = contract(own_rows, vectors)
    lower = vectors
    upper = vectors
    for reach in range(1, HALF + 1):
        lower = from_behind(lower, "vec", 1)
        upper = from_behind(upper, "vec", -1)
        triples[HALF - reach] = contract(scaled, lower)
        grams[HALF - reach] = contract(own_rows, lower)
        triples[HALF + reach] = contract(scaled, upper)
        grams[HALF + reach] = contract(own_rows, upper)
    triple_all = jnp.stack(triples).reshape(window, count, block_rows, block_rows)
    gram_all = jnp.stack(grams)
    gram_all = lax.all_gather(gram_all, "rep", axis=1, tiled=True)
    similarity = (triple_all - centre[None, :, None, None] * gram_all[:, None, :, :]) / math.sqrt(
        fields
    )
    return similarity.astype(jnp.bfloat16)


def solution(mesh):
    in_specs = (P("vec", None), P("rep", None))
    out_specs = P(None, "rep", "vec", None)
    return jax.shard_map(
        on_device, mesh=mesh, in_specs=in_specs, out_specs=out_specs, check_vma=False
    )
```

profile of v0, /device:TPU:0, one launch (start us, length us, event | category | flops | bytes accessed | tf_op | source)
XLA Modules:
  0.0 71.4 jit_solution(5123657337619987184)
XLA Ops:
  0.0 0.5 collective-permute-start
  0.5 4.0 %collective-permute-start.3 = (bf16[128,1024]{1,0:T(8,128)(2,1)}, bf16[128,1024]{1,0:T(8,128)(2,1)S(1)}, u32[]{:S(2)}, u32[]{:S(2)}) collective-permute-start(bf16[128,1024]{1,0:T(8,128)(2,1)} %param.2), channel_id=1, source_target_pairs={{4,0},{8,4},{12,8},{16,12},{20,16},{24,20},{28,24},{0,28},{5,1},{9... | collective-permute-start | bytes 786440 | tf_op jit(solution)/shard_map/ppermute | solution.py:13
  4.5 4.5 %collective-permute-done = bf16[128,1024]{1,0:T(8,128)(2,1)S(1)} collective-permute-done((bf16[128,1024]{1,0:T(8,128)(2,1)}, bf16[128,1024]{1,0:T(8,128)(2,1)S(1)}, u32[]{:S(2)}, u32[]{:S(2)}) %collective-permute-start) | collective-permute-done | bytes 262176 | tf_op jit(solution)/shard_map/ppermute | solution.py:13
  9.0 0.0 collective-permute-start.1
  9.0 0.7 subtract_bitcast_fusion
  9.7 0.0 collective-permute-done.3
  9.7 3.5 %collective-permute-start.4 = (bf16[128,1024]{1,0:T(8,128)(2,1)S(1)}, bf16[128,1024]{1,0:T(8,128)(2,1)S(1)}, u32[]{:S(2)}, u32[]{:S(2)}) collective-permute-start(bf16[128,1024]{1,0:T(8,128)(2,1)S(1)} %collective-permute-done.3), channel_id=1, source_target_pairs={{4,0},{8,4},{12,8},{16,12},{20,16},{24,20},{28,24},{0,28},{5,1},{9... | collective-permute-start | bytes 786440 | tf_op jit(solution)/shard_map/ppermute | solution.py:13
  13.2 3.5 %collective-permute-done.1 = bf16[128,1024]{1,0:T(8,128)(2,1)S(1)} collective-permute-done((bf16[128,1024]{1,0:T(8,128)(2,1)S(1)}, bf16[128,1024]{1,0:T(8,128)(2,1)S(1)}, u32[]{:S(2)}, u32[]{:S(2)}) %collective-permute-start.1) | collective-permute-done | bytes 262176 | tf_op jit(solution)/shard_map/ppermute | solution.py:13
  16.7 1.1 %fusion.56 = f32[8,1024]{1,0:T(8,128)S(1)} fusion(bf16[128,1024]{1,0:T(8,128)(2,1)} %param.2, s32[8]{0:T(128)S(1)} %subtract_bitcast_fusion), kind=kOutput, calls=%fused_computation.66 | convolution fusion | flops 2098176 | bytes 294944 | tf_op jit(solution)/shard_map/dot_general | solution.py:28
  17.8 1.0 %convert_element_type.21 = f32[128,1024]{1,0:T(8,128)S(1)} convert(bf16[128,1024]{1,0:T(8,128)(2,1)} %param.2) | non-fusion elementwise | flops 131072 | bytes 786432 | tf_op jit(solution)/shard_map/convert_element_type | solution.py:32
  18.8 29.4 %psum.7 = f32[8,1024]{1,0:T(8,128)S(1)} all-reduce(f32[8,1024]{1,0:T(8,128)S(1)} %fusion.56), channel_id=1, replica_groups=mesh['vec'=8,'rep'=4] {'vec'}, use_global_device_ids=true, to_apply=%region_0.0 | all-reduce | flops 8192 | bytes 65536 | tf_op jit(solution)/shard_map/psum | solution.py:29
  48.3 0.1 reduce_sum.9
  48.4 0.0 collective-permute-done.4
  48.4 0.1 collective-permute-start.5
  48.5 0.0 collective-permute-done.2
  48.5 1.0 %fusion.41 = f32[7,32,128]{2,1,0:T(8,128)S(1)} fusion(bf16[128,1024]{1,0:T(8,128)(2,1)S(1)} %collective-permute-done.2, bf16[128,1024]{1,0:T(8,128)(2,1)} %param.2, s32[]{:T(128)S(6)} %select_n.3), kind=kOutput, calls=%fused_computation.50 | convolution fusion | flops 8388607 | bytes 344068 | tf_op jit(solution)/shard_map/dot_general | solution.py:17
  49.5 1.0 %fusion.40 = f32[7,32,128]{2,1,0:T(8,128)S(1)} fusion(f32[7,32,128]{2,1,0:T(8,128)S(1)} %fusion.41, bf16[128,1024]{1,0:T(8,128)(2,1)S(1)} %collective-permute-done.1, bf16[128,1024]{1,0:T(8,128)(2,1)} %param.2, s32[]{:T(128)S(6)} %select_n.3), kind=kOutput, calls=%fused_computation.48 | convolution fusion | flops 8388608 | bytes 344068 | tf_op jit(solution)/shard_map/dot_general | solution.py:17
  50.5 1.0 %fusion.39 = f32[7,32,128]{2,1,0:T(8,128)S(1)} fusion(f32[7,32,128]{2,1,0:T(8,128)S(1)} %fusion.40, bf16[128,1024]{1,0:T(8,128)(2,1)S(1)} %collective-permute-done, bf16[128,1024]{1,0:T(8,128)(2,1)} %param.2, s32[]{:T(128)S(6)} %select_n.3), kind=kOutput, calls=%fused_computation.46 | convolution fusion | flops 8388608 | bytes 344068 | tf_op jit(solution)/shard_map/dot_general | solution.py:17
  51.6 1.2 %fusion.38 = f32[7,32,128]{2,1,0:T(8,128)S(1)} fusion(f32[7,32,128]{2,1,0:T(8,128)S(1)} %fusion.39, bf16[128,1024]{1,0:T(8,128)(2,1)} %param.2, s32[]{:T(128)S(6)} %select_n.3), kind=kOutput, calls=%fused_computation.44 | convolution fusion | flops 8388608 | bytes 344068 | tf_op jit(solution)/shard_map/dot_general | solution.py:17
  52.8 0.7 %fusion.22 = f32[7,8,128,128]{3,2,1,0:T(8,128)S(1)} fusion(f32[8,1024]{1,0:T(8,128)S(1)} %psum.7, f32[128,1024]{1,0:T(8,128)S(1)} %convert_element_type.21, bf16[128,1024]{1,0:T(8,128)(2,1)S(1)} %collective-permute-done.2), kind=kOutput, calls=%fused_computation.24 | convolution fusion | flops 270532608 | bytes 1343488 | tf_op jit(solution)/shard_map/dot_general | solution.py:17
  53.6 0.7 fusion.24
  54.3 0.7 fusion.26
  55.0 0.2 fusion.37
  55.2 0.2 fusion.36
  55.4 0.7 %fusion.28 = f32[7,8,128,128]{3,2,1,0:T(8,128)S(1)} fusion(f32[7,8,128,128]{3,2,1,0:T(8,128)S(1)} %fusion.26, f32[8,1024]{1,0:T(8,128)S(1)} %psum.7, f32[128,1024]{1,0:T(8,128)S(1)} %convert_element_type.21, bf16[128,1024]{1,0:T(8,128)(2,1)S(1)} %copy-done), kind=kOutput, calls=%fused_computation.30 | convolution fusion | flops 270532608 | bytes 1343488 | tf_op jit(solution)/shard_map/dot_general | solution.py:17
  56.1 0.0 collective-permute-done.5
  56.1 0.2 fusion.35
  56.3 11.0 %all_gather.3 = f32[7,128,128]{2,1,0:T(8,128)S(1)} all-gather(f32[7,32,128]{2,1,0:T(8,128)S(1)} %fusion.35), channel_id=1, replica_groups=mesh['vec'=8,'rep'=4] {'rep'}, dimensions={1}, use_global_device_ids=true | all-gather | bytes 573440 | tf_op jit(solution)/shard_map/all_gather | solution.py:53
  67.3 0.7 fusion.30
  68.0 0.7 fusion.32
  68.8 0.7 fusion.34
  69.5 1.9 %multiply_convert_fusion.8 = bf16[7,8,128,128]{3,2,1,0:T(8,128)(2,1)} fusion(f32[7,8,128,128]{3,2,1,0:T(8,128)S(1)} %fusion.34, f32[7,128,128]{2,1,0:T(8,128)S(1)} %all_gather.3, f32[8]{0:T(128)S(1)} %broadcast_multiply_fusion), kind=kLoop, calls=%fused_computation.8 | loop fusion | flops 3670016 | bytes 5963808 | tf_op jit(solution)/shard_map/convert_element_type | solution.py:57
  (4 shorter events, 0.0 us)
Async XLA Ops:
  0.0 9.0 %collective-permute-start = (bf16[128,1024]{1,0:T(8,128)(2,1)}, bf16[128,1024]{1,0:T(8,128)(2,1)S(1)}, u32[]{:S(2)}, u32[]{:S(2)}) collective-permute-start(bf16[128,1024]{1,0:T(8,128)(2,1)} %param.2), channel_id=1, source_target_pairs={{28,0},{0,4},{4,8},{8,12},{12,16},{16,20},{20,24},{24,28},{29,1},{... | collective-permute-start | bytes 786440 | tf_op jit(solution)/shard_map/ppermute | solution.py:13
  0.5 9.2 %collective-permute-start.3 = (bf16[128,1024]{1,0:T(8,128)(2,1)}, bf16[128,1024]{1,0:T(8,128)(2,1)S(1)}, u32[]{:S(2)}, u32[]{:S(2)}) collective-permute-start(bf16[128,1024]{1,0:T(8,128)(2,1)} %param.2), channel_id=1, source_target_pairs={{4,0},{8,4},{12,8},{16,12},{20,16},{24,20},{28,24},{0,28},{5,1},{9... | collective-permute-start | bytes 786440 | tf_op jit(solution)/shard_map/ppermute | solution.py:13
  9.0 7.7 %collective-permute-start.1 = (bf16[128,1024]{1,0:T(8,128)(2,1)S(1)}, bf16[128,1024]{1,0:T(8,128)(2,1)S(1)}, u32[]{:S(2)}, u32[]{:S(2)}) collective-permute-start(bf16[128,1024]{1,0:T(8,128)(2,1)S(1)} %collective-permute-done), channel_id=1, source_target_pairs={{28,0},{0,4},{4,8},{8,12},{12,16},{16,20},{20,24},{24,28},{29,1},{... | collective-permute-start | bytes 786440 | tf_op jit(solution)/shard_map/ppermute | solution.py:13
  9.7 38.7 %collective-permute-start.4 = (bf16[128,1024]{1,0:T(8,128)(2,1)S(1)}, bf16[128,1024]{1,0:T(8,128)(2,1)S(1)}, u32[]{:S(2)}, u32[]{:S(2)}) collective-permute-start(bf16[128,1024]{1,0:T(8,128)(2,1)S(1)} %collective-permute-done.3), channel_id=1, source_target_pairs={{4,0},{8,4},{12,8},{16,12},{20,16},{24,20},{28,24},{0,28},{5,1},{9... | collective-permute-start | bytes 786440 | tf_op jit(solution)/shard_map/ppermute | solution.py:13
  16.7 31.8 %collective-permute-start.2 = (bf16[128,1024]{1,0:T(8,128)(2,1)S(1)}, bf16[128,1024]{1,0:T(8,128)(2,1)S(1)}, u32[]{:S(2)}, u32[]{:S(2)}) collective-permute-start(bf16[128,1024]{1,0:T(8,128)(2,1)S(1)} %collective-permute-done.1), channel_id=1, source_target_pairs={{28,0},{0,4},{4,8},{8,12},{12,16},{16,20},{20,24},{24,28},{29,1},{... | collective-permute-start | bytes 786440 | tf_op jit(solution)/shard_map/ppermute | solution.py:13
  48.4 7.7 %collective-permute-start.5 = (bf16[128,1024]{1,0:T(8,128)(2,1)S(1)}, bf16[128,1024]{1,0:T(8,128)(2,1)S(1)}, u32[]{:S(2)}, u32[]{:S(2)}) collective-permute-start(bf16[128,1024]{1,0:T(8,128)(2,1)S(1)} %collective-permute-done.4), channel_id=1, source_target_pairs={{4,0},{8,4},{12,8},{16,12},{20,16},{24,20},{28,24},{0,28},{5,1},{9... | collective-permute-start | bytes 786440 | tf_op jit(solution)/shard_map/ppermute | solution.py:13
  52.8 2.2 %copy-start = (bf16[128,1024]{1,0:T(8,128)(2,1)S(1)}, bf16[128,1024]{1,0:T(8,128)(2,1)}, u32[]{:S(2)}) copy-start(bf16[128,1024]{1,0:T(8,128)(2,1)} %param.2) | copy-start | bytes 786436
where the time goes:
time: 71.7 us; the launch traced here: 71.4 us
  blocking collectives  40.5 us (56%)
  matrix products  11 us (15%)
  starting transfers between devices  8.13 us (11%)
  waiting for transfers between devices  7.96 us (11%)
  other arithmetic  3.69 us (5%)
    psum x1, blocking collectives, on_device(): pivots = lax.psum(local_rows, 'vec')  29.4 us
    all_gather x1, blocking collectives, on_device(): gram_all = lax.all_gather(gram_all, 'rep', axis=1, tiled=True)  11 us
    dot_general x14, matrix products, contract(): lax.dot_general(left, right, (((1,), (1,)), ((), ())), preferred_element_...  9.87 us
    ppermute x6, starting transfers between devices, from_behind(): return lax.ppermute(block, axis, route)  8.13 us
    ppermute x6, waiting for transfers between devices, from_behind(): return lax.ppermute(block, axis, route)  7.96 us
    convert_element_type x1, other arithmetic, on_device(): return similarity.astype(jnp.bfloat16)  1.9 us
  transfers between devices with their start and end apart: 6, of which 2 were waited for; matrix products, arithmetic and copies ran while one was open for 15% of the time, Pallas kernels for 0%

commit v1 on v0

--- a/solution.py
+++ b/solution.py
@@ -50,7 +50,12 @@
         grams[HALF + reach] = contract(own_rows, upper)
     triple_all = jnp.stack(triples).reshape(window, count, block_rows, block_rows)
     gram_all = jnp.stack(grams)
-    gram_all = lax.all_gather(gram_all, "rep", axis=1, tiled=True)
+    ring = [gram_all]
+    for hop in range(3):
+        ring.append(lax.ppermute(ring[-1], "rep", [(dev, (dev + 1) % 4) for dev in range(4)]))
+    gram_all = jnp.roll(
+        jnp.concatenate(ring[::-1], axis=1), (lax.axis_index("rep") + 1) * ring[0].shape[1], axis=1
+    )
     similarity = (triple_all - centre[None, :, None, None] * gram_all[:, None, :, :]) / math.sqrt(
         fields
     )

time: 71.7 us -> 77.7 us (1.084)
  waiting for transfers between devices: 7.96 us -> 21.3 us
  blocking collectives: 40.5 us -> 29.4 us
  starting transfers between devices: 8.13 us -> 11.4 us
    ppermute x0 -> x3, waiting for transfers between devices: none -> 13.4 us  [on_device(): lax.ppermute(ring[-1], 'rep', [(dev, (dev + 1) % 4) for dev in range(4)])]
    all_gather x1 -> x0, blocking collectives: 11 us -> none  [on_device(): gram_all = lax.all_gather(gram_all, 'rep', axis=1, tiled=True)]
    ppermute x0 -> x3, starting transfers between devices: none -> 3.27 us  [on_device(): lax.ppermute(ring[-1], 'rep', [(dev, (dev + 1) % 4) for dev in range(4)])]
  transfers between devices with their start and end apart: 6 -> 9, of which waited for: 2 -> 5; matrix products, arithmetic and copies ran while one was open for 15% -> 16% of each run, Pallas kernels for 0% -> 0%
where the time goes in v1:
time: 77.7 us; the launch traced here: 77.3 us
  blocking collectives  29.4 us (38%)
  waiting for transfers between devices  21.3 us (27%)
  starting transfers between devices  11.4 us (15%)
  matrix products  11 us (14%)
  other arithmetic  3.69 us (5%)
    psum x1, blocking collectives, on_device(): pivots = lax.psum(local_rows, 'vec')  29.4 us
    ppermute x3, waiting for transfers between devices, on_device(): lax.ppermute(ring[-1], 'rep', [(dev, (dev + 1) % 4) for dev in range(4)])  13.4 us
    dot_general x14, matrix products, contract(): lax.dot_general(left, right, (((1,), (1,)), ((), ())), preferred_element_...  9.87 us
    ppermute x6, starting transfers between devices, from_behind(): return lax.ppermute(block, axis, route)  8.13 us
    ppermute x6, waiting for transfers between devices, from_behind(): return lax.ppermute(block, axis, route)  7.96 us
    ppermute x3, starting transfers between devices, on_device(): lax.ppermute(ring[-1], 'rep', [(dev, (dev + 1) % 4) for dev in range(4)])  3.27 us
    convert_element_type x1, other arithmetic, on_device(): return similarity.astype(jnp.bfloat16)  1.9 us
  transfers between devices with their start and end apart: 9, of which 5 were waited for; matrix products, arithmetic and copies ran while one was open for 16% of the time, Pallas kernels for 0%

profile of v1, /device:TPU:0, one launch (start us, length us, event | category | flops | bytes accessed | tf_op | source)
XLA Modules:
  0.0 77.3 jit_solution(18026916061641735386)
XLA Ops:
  0.0 0.5 collective-permute-start
  0.5 4.0 %collective-permute-start.3 = (bf16[128,1024]{1,0:T(8,128)(2,1)}, bf16[128,1024]{1,0:T(8,128)(2,1)S(1)}, u32[]{:S(2)}, u32[]{:S(2)}) collective-permute-start(bf16[128,1024]{1,0:T(8,128)(2,1)} %param.2), channel_id=1, source_target_pairs={{4,0},{8,4},{12,8},{16,12},{20,16},{24,20},{28,24},{0,28},{5,1},{9... | collective-permute-start | bytes 786440 | tf_op jit(solution)/shard_map/ppermute | solution.py:13
  4.5 4.5 %collective-permute-done = bf16[128,1024]{1,0:T(8,128)(2,1)S(1)} collective-permute-done((bf16[128,1024]{1,0:T(8,128)(2,1)}, bf16[128,1024]{1,0:T(8,128)(2,1)S(1)}, u32[]{:S(2)}, u32[]{:S(2)}) %collective-permute-start) | collective-permute-done | bytes 262176 | tf_op jit(solution)/shard_map/ppermute | solution.py:13
  9.0 0.7 subtract_bitcast_fusion
  9.7 0.0 collective-permute-done.3
  9.7 3.5 %collective-permute-start.4 = (bf16[128,1024]{1,0:T(8,128)(2,1)S(1)}, bf16[128,1024]{1,0:T(8,128)(2,1)S(1)}, u32[]{:S(2)}, u32[]{:S(2)}) collective-permute-start(bf16[128,1024]{1,0:T(8,128)(2,1)S(1)} %collective-permute-done.3), channel_id=1, source_target_pairs={{4,0},{8,4},{12,8},{16,12},{20,16},{24,20},{28,24},{0,28},{5,1},{9... | collective-permute-start | bytes 786440 | tf_op jit(solution)/shard_map/ppermute | solution.py:13
  13.2 3.5 %collective-permute-done.1 = bf16[128,1024]{1,0:T(8,128)(2,1)S(1)} collective-permute-done((bf16[128,1024]{1,0:T(8,128)(2,1)S(1)}, bf16[128,1024]{1,0:T(8,128)(2,1)S(1)}, u32[]{:S(2)}, u32[]{:S(2)}) %collective-permute-start.1) | collective-permute-done | bytes 262176 | tf_op jit(solution)/shard_map/ppermute | solution.py:13
  16.7 1.1 %fusion.49 = f32[8,1024]{1,0:T(8,128)S(1)} fusion(bf16[128,1024]{1,0:T(8,128)(2,1)} %param.2, s32[8]{0:T(128)S(1)} %subtract_bitcast_fusion), kind=kOutput, calls=%fused_computation.86 | convolution fusion | flops 2098176 | bytes 294944 | tf_op jit(solution)/shard_map/dot_general | solution.py:28
  17.8 1.0 %convert_element_type.21 = f32[128,1024]{1,0:T(8,128)S(1)} convert(bf16[128,1024]{1,0:T(8,128)(2,1)} %param.2) | non-fusion elementwise | flops 131072 | bytes 786432 | tf_op jit(solution)/shard_map/convert_element_type | solution.py:32
  18.9 29.4 %psum.7 = f32[8,1024]{1,0:T(8,128)S(1)} all-reduce(f32[8,1024]{1,0:T(8,128)S(1)} %fusion.49), channel_id=1, replica_groups=mesh['vec'=8,'rep'=4] {'vec'}, use_global_device_ids=true, to_apply=%region_0.0 | all-reduce | flops 8192 | bytes 65536 | tf_op jit(solution)/shard_map/psum | solution.py:29
  48.3 0.1 reduce_sum.9
  48.4 0.1 collective-permute-start.5
  48.5 1.0 %constant_dynamic-update-slice_fusion.6 = (f32[7,32,128]{2,1,0:T(8,128)S(1)}, f32[1,32,128]{2,1,0:T(8,128)S(1)}) fusion(bf16[128,1024]{1,0:T(8,128)(2,1)S(1)} %collective-permute-done.2, bf16[128,1024]{1,0:T(8,128)(2,1)} %param.2, s32[]{:T(128)S(6)} %select_n.16), kind=kOutput, calls=%fused_computation.57 | convolution fusion | flops 8388607 | bytes 360452 | tf_op jit(solution)/shard_map/dot_general | solution.py:17
  49.5 1.0 %constant_dynamic-update-slice_fusion.5 = (f32[7,32,128]{2,1,0:T(8,128)S(1)}, f32[1,32,128]{2,1,0:T(8,128)S(1)}) fusion(f32[7,32,128]{2,1,0:T(8,128)S(1)} %get-tuple-element.5, bf16[128,1024]{1,0:T(8,128)(2,1)S(1)} %collective-permute-done.1, bf16[128,1024]{1,0:T(8,128)(2,1)} %param.2, s32[]{:T(128)S(6)} %select_n.16), kind=kOutput, calls=%fused_computation.56 | convolution fusion | flops 8388608 | bytes 360452 | tf_op jit(solution)/shard_map/dot_general | solution.py:17
  50.6 1.0 %constant_dynamic-update-slice_fusion.4 = (f32[7,32,128]{2,1,0:T(8,128)S(1)}, f32[1,32,128]{2,1,0:T(8,128)S(1)}) fusion(f32[7,32,128]{2,1,0:T(8,128)S(1)} %get-tuple-element.7, bf16[128,1024]{1,0:T(8,128)(2,1)S(1)} %collective-permute-done, bf16[128,1024]{1,0:T(8,128)(2,1)} %param.2, s32[]{:T(128)S(6)} %select_n.16), kind=kOutput, calls=%fused_computation.55 | convolution fusion | flops 8388608 | bytes 360452 | tf_op jit(solution)/shard_map/dot_general | solution.py:17
  51.6 1.2 %constant_dynamic-update-slice_fusion.3 = (f32[7,32,128]{2,1,0:T(8,128)S(1)}, f32[1,32,128]{2,1,0:T(8,128)S(1)}) fusion(f32[7,32,128]{2,1,0:T(8,128)S(1)} %get-tuple-element.9, bf16[128,1024]{1,0:T(8,128)(2,1)} %param.2, s32[]{:T(128)S(6)} %select_n.16), kind=kOutput, calls=%fused_computation.54 | convolution fusion | flops 8388608 | bytes 360452 | tf_op jit(solution)/shard_map/dot_general | solution.py:17
  52.8 0.7 fusion.22
  53.6 0.7 fusion.24
  54.3 0.7 fusion.26
  55.0 0.2 constant_dynamic-update-slice_fusion.2
  55.2 0.2 constant_dynamic-update-slice_fusion.1
  55.4 0.7 fusion.28
  56.1 0.2 constant_dynamic-update-slice_fusion
  56.3 2.5 %collective-permute-start.6 = (f32[7,32,128]{2,1,0:T(8,128)S(1)}, f32[7,32,128]{2,1,0:T(8,128)S(1)}, u32[]{:S(2)}, u32[]{:S(2)}) collective-permute-start(f32[7,32,128]{2,1,0:T(8,128)S(1)} %get-tuple-element.17), channel_id=1, source_target_pairs={{0,1},{1,2},{2,3},{3,0},{4,5},{5,6},{6,7},{7,4},{8,9},{9,10},{10,1... | collective-permute-start | bytes 344072 | tf_op jit(solution)/shard_map/ppermute | solution.py:55
  58.8 0.7 fusion.30
  59.5 4.0 %collective-permute-done.6 = f32[7,32,128]{2,1,0:T(8,128)S(1)} collective-permute-done((f32[7,32,128]{2,1,0:T(8,128)S(1)}, f32[7,32,128]{2,1,0:T(8,128)S(1)}, u32[]{:S(2)}, u32[]{:S(2)}) %collective-permute-start.6) | collective-permute-done | bytes 114720 | tf_op jit(solution)/shard_map/ppermute | solution.py:55
  63.5 0.8 %collective-permute-start.7 = (f32[7,32,128]{2,1,0:T(8,128)S(1)}, f32[7,32,128]{2,1,0:T(8,128)S(1)}, u32[]{:S(2)}, u32[]{:S(2)}) collective-permute-start(f32[7,32,128]{2,1,0:T(8,128)S(1)} %collective-permute-done.6), channel_id=1, source_target_pairs={{0,1},{1,2},{2,3},{3,0},{4,5},{5,6},{6,7},{7,4},{8,9},{9,10},{10,1... | collective-permute-start | bytes 344072 | tf_op jit(solution)/shard_map/ppermute | solution.py:55
  64.3 0.7 fusion.32
  65.0 4.3 %collective-permute-done.7 = f32[7,32,128]{2,1,0:T(8,128)S(1)} collective-permute-done((f32[7,32,128]{2,1,0:T(8,128)S(1)}, f32[7,32,128]{2,1,0:T(8,128)S(1)}, u32[]{:S(2)}, u32[]{:S(2)}) %collective-permute-start.7) | collective-permute-done | bytes 114720 | tf_op jit(solution)/shard_map/ppermute | solution.py:55
  69.4 0.7 fusion.34
  70.1 5.0 %collective-permute-done.8 = f32[7,32,128]{2,1,0:T(8,128)S(1)} collective-permute-done((f32[7,32,128]{2,1,0:T(8,128)S(1)}, f32[7,32,128]{2,1,0:T(8,128)S(1)}, u32[]{:S(2)}, u32[]{:S(2)}) %collective-permute-start.8) | collective-permute-done | bytes 114720 | tf_op jit(solution)/shard_map/ppermute | solution.py:55
  75.4 1.9 %multiply_convert_fusion.8 = bf16[7,8,128,128]{3,2,1,0:T(8,128)(2,1)} fusion(f32[7,8,128,128]{3,2,1,0:T(8,128)S(1)} %fusion.34, f32[7,128,128]{2,1,0:T(8,128)S(1)} %constant_dynamic-slice_fusion, f32[8]{0:T(128)S(1)} %broadcast_multiply_fusion), kind=kLoop, calls=%fused_computation.8 | loop fusion | flops 3670016 | bytes 5963808 | tf_op jit(solution)/shard_map/convert_element_type | solution.py:62
  (30 shorter events, 0.2 us)
Async XLA Ops:
  0.0 9.0 %collective-permute-start = (bf16[128,1024]{1,0:T(8,128)(2,1)}, bf16[128,1024]{1,0:T(8,128)(2,1)S(1)}, u32[]{:S(2)}, u32[]{:S(2)}) collective-permute-start(bf16[128,1024]{1,0:T(8,128)(2,1)} %param.2), channel_id=1, source_target_pairs={{28,0},{0,4},{4,8},{8,12},{12,16},{16,20},{20,24},{24,28},{29,1},{... | collective-permute-start | bytes 786440 | tf_op jit(solution)/shard_map/ppermute | solution.py:13
  0.5 9.2 %collective-permute-start.3 = (bf16[128,1024]{1,0:T(8,128)(2,1)}, bf16[128,1024]{1,0:T(8,128)(2,1)S(1)}, u32[]{:S(2)}, u32[]{:S(2)}) collective-permute-start(bf16[128,1024]{1,0:T(8,128)(2,1)} %param.2), channel_id=1, source_target_pairs={{4,0},{8,4},{12,8},{16,12},{20,16},{24,20},{28,24},{0,28},{5,1},{9... | collective-permute-start | bytes 786440 | tf_op jit(solution)/shard_map/ppermute | solution.py:13
  9.0 7.7 %collective-permute-start.1 = (bf16[128,1024]{1,0:T(8,128)(2,1)S(1)}, bf16[128,1024]{1,0:T(8,128)(2,1)S(1)}, u32[]{:S(2)}, u32[]{:S(2)}) collective-permute-start(bf16[128,1024]{1,0:T(8,128)(2,1)S(1)} %collective-permute-done), channel_id=1, source_target_pairs={{28,0},{0,4},{4,8},{8,12},{12,16},{16,20},{20,24},{24,28},{29,1},{... | collective-permute-start | bytes 786440 | tf_op jit(solution)/shard_map/ppermute | solution.py:13
  9.7 38.8 %collective-permute-start.4 = (bf16[128,1024]{1,0:T(8,128)(2,1)S(1)}, bf16[128,1024]{1,0:T(8,128)(2,1)S(1)}, u32[]{:S(2)}, u32[]{:S(2)}) collective-permute-start(bf16[128,1024]{1,0:T(8,128)(2,1)S(1)} %collective-permute-done.3), channel_id=1, source_target_pairs={{4,0},{8,4},{12,8},{16,12},{20,16},{24,20},{28,24},{0,28},{5,1},{9... | collective-permute-start | bytes 786440 | tf_op jit(solution)/shard_map/ppermute | solution.py:13
  16.7 31.8 %collective-permute-start.2 = (bf16[128,1024]{1,0:T(8,128)(2,1)S(1)}, bf16[128,1024]{1,0:T(8,128)(2,1)S(1)}, u32[]{:S(2)}, u32[]{:S(2)}) collective-permute-start(bf16[128,1024]{1,0:T(8,128)(2,1)S(1)} %collective-permute-done.1), channel_id=1, source_target_pairs={{28,0},{0,4},{4,8},{8,12},{12,16},{16,20},{20,24},{24,28},{29,1},{... | collective-permute-start | bytes 786440 | tf_op jit(solution)/shard_map/ppermute | solution.py:13
  48.4 7.7 %collective-permute-start.5 = (bf16[128,1024]{1,0:T(8,128)(2,1)S(1)}, bf16[128,1024]{1,0:T(8,128)(2,1)S(1)}, u32[]{:S(2)}, u32[]{:S(2)}) collective-permute-start(bf16[128,1024]{1,0:T(8,128)(2,1)S(1)} %collective-permute-done.4), channel_id=1, source_target_pairs={{4,0},{8,4},{12,8},{16,12},{20,16},{24,20},{28,24},{0,28},{5,1},{9... | collective-permute-start | bytes 786440 | tf_op jit(solution)/shard_map/ppermute | solution.py:13
  52.8 2.2 %copy-start = (bf16[128,1024]{1,0:T(8,128)(2,1)S(1)}, bf16[128,1024]{1,0:T(8,128)(2,1)}, u32[]{:S(2)}) copy-start(bf16[128,1024]{1,0:T(8,128)(2,1)} %param.2) | copy-start | bytes 786436
  56.3 7.2 %collective-permute-start.6 = (f32[7,32,128]{2,1,0:T(8,128)S(1)}, f32[7,32,128]{2,1,0:T(8,128)S(1)}, u32[]{:S(2)}, u32[]{:S(2)}) collective-permute-start(f32[7,32,128]{2,1,0:T(8,128)S(1)} %get-tuple-element.17), channel_id=1, source_target_pairs={{0,1},{1,2},{2,3},{3,0},{4,5},{5,6},{6,7},{7,4},{8,9},{9,10},{10,1... | collective-permute-start | bytes 344072 | tf_op jit(solution)/shard_map/ppermute | solution.py:55
  63.5 5.9 %collective-permute-start.7 = (f32[7,32,128]{2,1,0:T(8,128)S(1)}, f32[7,32,128]{2,1,0:T(8,128)S(1)}, u32[]{:S(2)}, u32[]{:S(2)}) collective-permute-start(f32[7,32,128]{2,1,0:T(8,128)S(1)} %collective-permute-done.6), channel_id=1, source_target_pairs={{0,1},{1,2},{2,3},{3,0},{4,5},{5,6},{6,7},{7,4},{8,9},{9,10},{10,1... | collective-permute-start | bytes 344072 | tf_op jit(solution)/shard_map/ppermute | solution.py:55
  69.4 5.7 %collective-permute-start.8 = (f32[7,32,128]{2,1,0:T(8,128)S(1)}, f32[7,32,128]{2,1,0:T(8,128)S(1)}, u32[]{:S(2)}, u32[]{:S(2)}) collective-permute-start(f32[7,32,128]{2,1,0:T(8,128)S(1)} %collective-permute-done.7), channel_id=1, source_target_pairs={{0,1},{1,2},{2,3},{3,0},{4,5},{5,6},{6,7},{7,4},{8,9},{9,10},{10,1... | collective-permute-start | bytes 344072 | tf_op jit(solution)/shard_map/ppermute | solution.py:55
